TPU v7x, 128 devices: a whole 4x4x4 slice. The times are simulated.
128 devices in a mesh: sec: 2 (over y_hi), dev: 32 (over z, x, core), tp: 2 (over y_lo).
Axes of the slice: x: 4, y: 4 (y_hi: 2, y_lo: 2; y = y_hi * 2 + y_lo), z: 4, core: 2. Of those that a mesh axis runs over, the one named last changes fastest.
Arguments:
- queries: bfloat16 [512, 8192], P(('sec', 'dev'), 'tp'), may hold values from -6 to 6
- new_keys: bfloat16 [512, 1024], P(('sec', 'dev'), 'tp'), may hold values from -6 to 6
- token_values: bfloat16 [512, 1024], P(('sec', 'dev'), 'tp'), may hold values from -6 to 6
- key_cache: bfloat16 [512, 256, 1024], P(('sec', 'dev'), None, 'tp'), may hold values from -6 to 6
- stored_values: bfloat16 [512, 256, 1024], P(('sec', 'dev'), None, 'tp'), may hold values from -6 to 6
- cache_lengths: int32 [512], P(('sec', 'dev')), may hold values from 1 to 256, 65536 in all
- residual: bfloat16 [512, 8192], P(('sec', 'dev', 'tp')), may hold values from -6 to 6
- norm_gain: float32 [8192], replicated, may hold values from 0.25 to 1.75
- active: int32 [512, 16], P(('sec', 'dev', 'tp')), may hold values from 0 to 127, all different within a row; in each aligned block of 4 rows (0 to 3, 4 to 7, ...) at most 3 rows name the same one
- gate_weight: bfloat16 [8192, 16384], P(None, ('sec', 'dev', 'tp')), may hold values from -0.0625 to 0.0625
- up_weight: bfloat16 [8192, 16384], P(None, ('sec', 'dev', 'tp')), may hold values from -0.0625 to 0.0625
- down_weight: bfloat16 [16384, 8192], P(('sec', 'dev', 'tp')), may hold values from -0.125 to 0.125
Outputs:
- layer_out: bfloat16 [512, 8192], P(('sec', 'dev', 'tp'))
Inputs may be any that keep to these rules, and one draw needn't show every extreme that they name: `cache_lengths`: the largest length is 256 in every draw. `active`: the bundles of one row are distinct. Among the 4 rows of one device (aligned blocks of rows), no bundle is named by more than 3 rows, and some bundle reaches 3.
All inputs are finite; a program needn't handle non-finite values. No bound on the sum of `cache_lengths` on one device may be relied on, other than what follows from the above.
Results may differ from a plain program's by a relative error of at most 0.007.
Values may be sent and summed in bfloat16 or wider, within the bound.
A program may use at most 128 MiB of HBM per device.

v0:
```python
import jax
import jax.numpy as jnp
from jax import lax
from jax.sharding import PartitionSpec as P

HEAD_SIZE = 128
CACHE_POSITIONS = 256
epsilon = 1e-05


def attend(queries, new_keys, token_values, key_cache, stored_values, cache_lengths):
    request_count, query_width = queries.shape
    kv_width = new_keys.shape[1]
    kv_heads = kv_width // HEAD_SIZE
    group_width = query_width // kv_width
    scaling = HEAD_SIZE ** (-0.5)
    grouped = queries.reshape(request_count, kv_heads, group_width, HEAD_SIZE)
    cached_keys = key_cache.reshape(request_count, CACHE_POSITIONS, kv_heads, HEAD_SIZE)
    cached_values = stored_values.reshape(request_count, CACHE_POSITIONS, kv_heads, HEAD_SIZE)
    scores = (
        jnp.einsum("rkgd,rckd->rkgc", grouped, cached_keys, preferred_element_type=jnp.float32)
        * scaling
    )
    visible = jnp.arange(CACHE_POSITIONS, dtype=jnp.int32)[None, :] < cache_lengths[:, None]
    scores = jnp.where(visible[:, None, None, :], scores, -jnp.inf)
    fresh_keys = new_keys.reshape(request_count, kv_heads, HEAD_SIZE)
    fresh_score = (
        jnp.einsum("rkgd,rkd->rkg", grouped, fresh_keys, preferred_element_type=jnp.float32)
        * scaling
    )
    highest = jnp.maximum(jnp.max(scores, axis=-1), fresh_score)
    weights_cache = jnp.exp(scores - highest[..., None])
    weight_fresh = jnp.exp(fresh_score - highest)
    denominator = jnp.sum(weights_cache, axis=-1) + weight_fresh
    probs_cache = (weights_cache / denominator[..., None]).astype(jnp.bfloat16)
    prob_fresh = (weight_fresh / denominator).astype(jnp.bfloat16)
    blended = jnp.einsum(
        "rkgc,rckd->rkgd", probs_cache, cached_values, preferred_element_type=jnp.float32
    )
    fresh_values = token_values.reshape(request_count, kv_heads, 1, HEAD_SIZE).astype(jnp.float32)
    blended = blended + prob_fresh[..., None].astype(jnp.float32) * fresh_values
    return blended.reshape(request_count, query_width).astype(jnp.bfloat16)


def feed_forward(row_block, gate_weight, up_weight, selected):
    gate_value = jnp.dot(row_block, gate_weight, preferred_element_type=jnp.float32)
    up_value = jnp.dot(row_block, up_weight, preferred_element_type=jnp.float32)
    return (jax.nn.relu(gate_value) * up_value * selected).astype(jnp.bfloat16)


def shards(
    queries,
    new_keys,
    token_values,
    key_cache,
    stored_values,
    cache_lengths,
    residual,
    norm_gain,
    active,
    gate_weight,
    up_weight,
    down_weight,
):
    context = attend(queries, new_keys, token_values, key_cache, stored_values, cache_lengths)
    context = lax.all_to_all(context, "tp", split_axis=0, concat_axis=1, tiled=True)
    stream = residual.astype(jnp.float32) + context.astype(jnp.float32)
    mean_square = jnp.mean(stream * stream, axis=1, keepdims=True)
    normed = (stream * lax.rsqrt(mean_square + epsilon) * norm_gain[None, :]).astype(jnp.bfloat16)
    axes = ("sec", "dev", "tp")
    bundle = lax.axis_index(axes)
    named = jnp.any(active[:, :, None] == jnp.arange(128, dtype=jnp.int32)[None, None, :], axis=1)
    packed = jnp.concatenate([normed, named.astype(jnp.bfloat16)], axis=1)
    gathered = lax.all_gather(packed, axes, axis=0, tiled=True)
    rows = gathered[:, :8192]
    wanted = jnp.sum(
        jnp.where(jnp.arange(128)[None, :] == bundle, gathered[:, 8192:].astype(jnp.float32), 0.0),
        axis=1,
        keepdims=True,
    )
    hidden = feed_forward(rows, gate_weight, up_weight, wanted)
    terms = jnp.dot(hidden, down_weight, preferred_element_type=jnp.float32).astype(jnp.bfloat16)
    terms = terms.reshape(128, 32, 1024)
    update = lax.psum_scatter(terms, axes, scatter_dimension=0, tiled=False).reshape(4, 8192)
    return (stream + update.astype(jnp.float32)).astype(jnp.bfloat16)


def solution(mesh):
    return jax.shard_map(
        shards,
        mesh=mesh,
        in_specs=(
            P(("sec", "dev"), "tp"),
            P(("sec", "dev"), "tp"),
            P(("sec", "dev"), "tp"),
            P(("sec", "dev"), None, "tp"),
            P(("sec", "dev"), None, "tp"),
            P(("sec", "dev")),
            P(("sec", "dev", "tp"), None),
            P(),
            P(("sec", "dev", "tp"), None),
            P(None, ("sec", "dev", "tp")),
            P(None, ("sec", "dev", "tp")),
            P(("sec", "dev", "tp"), None),
        ),
        out_specs=P(("sec", "dev", "tp"), None),
        check_vma=False,
    )
```

profile of v0, /device:TPU:0, one launch (start us, length us, event | category | flops | bytes accessed | tf_op | source)
XLA Modules:
  0.0 1051.2 jit_solution(6356441522327722411)
XLA Ops:
  6.5 0.9 iota_compare_fusion.1
  7.4 0.8 bitcast_convert_fusion
  8.2 1.0 fusion.41
  9.2 2.4 fusion.49
  11.6 0.2 fusion.36
  11.9 0.5 fusion.33
  12.4 0.7 convert_element_type.71
  13.0 3.3 all-to-all-start
  16.3 0.0 all-gather.3.cloned.1.call-start
  16.4 0.1 fusion.44
  16.5 3.9 all-to-all-done
  20.5 0.2 multiply_reduce_fusion
  20.7 0.1 multiply_convert_fusion
  20.8 0.6 maximum_bitcast_fusion
  21.4 0.0 reduce-scatter.2.cloned.1.call-start
  21.5 311.8 %all-gather.3.cloned.1.call-done = bf16[128,4,8320]{2,1,0:T(4,128)(2,1)} async-done(((bf16[1,4,8320]{2,1,0:T(4,128)(2,1)}), bf16[128,4,8320]{2,1,0:T(4,128)(2,1)}) %all-gather.3.cloned.1.call-update) | async-done | bytes 8519696 | tf_op jit(solution)/shard_map/all_gather | solution.py:74
  333.3 12.6 %reshape.81 = bf16[512,8320]{1,0:T(8,128)(2,1)} reshape(bf16[128,4,8320]{2,1,0:T(4,128)(2,1)} %all-gather.3.cloned.1.call-done) | data formatting | bytes 17039360
  345.9 1.0 select_reduce_fusion
  346.9 6.3 fusion
  353.2 17.2 %convolution_convert_fusion = bf16[512,8192]{1,0:T(8,128)(2,1)} fusion(bf16[128,8192]{1,0:T(8,128)(2,1)S(1)} %copy-done, f32[512,128]{1,0:T(8,128)S(1)} %fusion, bf16[8192,128]{1,0:T(8,128)(2,1)} %param.21, bf16[512,8320]{1,0:T(8,128)(2,1)} %reshape.81, f32[512]{0:T(512)S(1)} %select_reduce_fusion), kind=kOutput, calls=%fused_computation | convolution fusion | flops 2151940096 | bytes 21235712 | tf_op jit(solution)/shard_map/dot_general | solution.py:82
  370.4 13.5 %reshape.76 = bf16[128,32,1024]{2,1,0:T(8,128)(2,1)} reshape(bf16[512,8192]{1,0:T(8,128)(2,1)} %convolution_convert_fusion) | data formatting | bytes 16777216 | tf_op jit(solution)/shard_map/reshape | solution.py:83
  383.9 658.9 %reduce-scatter.2.cloned.1.call-done = bf16[1,32,1024]{2,1,0:T(8,128)(2,1)} async-done(((bf16[128,32,1024]{2,1,0:T(8,128)(2,1)}), bf16[1,32,1024]{2,1,0:T(8,128)(2,1)}) %reduce-scatter.2.cloned.1.call-update) | async-done | bytes 65552 | tf_op jit(solution)/shard_map/reduce_scatter | solution.py:84
  1042.8 0.9 reshape.79
  1043.7 0.7 add_convert_fusion
  (19 shorter events, 0.1 us)
Async XLA Ops:
  6.5 346.7 %copy-start = (bf16[128,8192]{1,0:T(8,128)(2,1)S(1)}, bf16[128,8192]{1,0:T(8,128)(2,1)}, u32[]{:S(2)}) copy-start(bf16[128,8192]{1,0:T(8,128)(2,1)} %param.23) | copy-start | bytes 6291460
  6.5 5.4 copy-start.4
  11.6 4.8 copy-start.3
  11.8 8.6 copy-start.1
  11.9 8.8 copy-start.2
  13.0 7.4 all-to-all-start
  16.3 317.0 %all-gather.3.cloned.1.call-start = ((), (), s32[]{:S(2)}) async-start(), calls=%async_computation.3 | async-start | bytes 8586240 | tf_op jit(solution)/shard_map/all_gather | solution.py:74
  21.4 1021.3 %reduce-scatter.2.cloned.1.call-start = ((), (), s32[]{:S(2)}) async-start(), calls=%async_computation.2 | async-start | bytes 8454144 | tf_op jit(solution)/shard_map/reduce_scatter | solution.py:84
Sparse Core Ops, SparseCore 0:
  21.6 311.6 all-gather.2
  384.0 658.6 reduce-scatter.1
where the time goes:
time: 1050 us
  waiting for transfers between devices  975 us (93%)
  local copies, waits for them, and re-layouts  27.7 us (3%)
  matrix products  27.3 us (3%)
  between operations  13.5 us (1%)
    reduce_scatter x1, waiting for transfers between devices, shards(): lax.psum_scatter(terms, axes, scatter_dimension=0, tiled=False)  659 us
    all_gather x1, waiting for transfers between devices, shards(): gathered = lax.all_gather(packed, axes, axis=0, tiled=True)  312 us
  transfers between devices with their start and end apart: 3, of which 3 were waited for; matrix products, arithmetic and copies ran while one was open for 0% of the time, Pallas kernels for 0%

commit v1 on v0

--- a/solution.py
+++ b/solution.py
@@ -71,7 +71,9 @@
     bundle = lax.axis_index(axes)
     named = jnp.any(active[:, :, None] == jnp.arange(128, dtype=jnp.int32)[None, None, :], axis=1)
     packed = jnp.concatenate([normed, named.astype(jnp.bfloat16)], axis=1)
-    gathered = lax.all_gather(packed, axes, axis=0, tiled=True)
+    gathered = jnp.concatenate(
+        lax.all_to_all(jnp.stack([packed] * lax.axis_size(axes)), axes, 0, 0), axis=0
+    )
     rows = gathered[:, :8192]
     wanted = jnp.sum(
         jnp.where(jnp.arange(128)[None, :] == bundle, gathered[:, 8192:].astype(jnp.float32), 0.0),

time: 1050 us -> 871 us (0.83)
  waiting for transfers between devices: 975 us -> 777 us
  starting transfers between devices: 3.38 us -> 15 us
    all_gather x1 -> x0, waiting for transfers between devices: 312 us -> none  [shards(): gathered = lax.all_gather(packed, axes, axis=0, tiled=True)]
    all_to_all x0 -> x1, waiting for transfers between devices: none -> 103 us  [shards(): lax.all_to_all(jnp.stack([packed] * lax.axis_size(axes)), axes, 0, 0)]
    reshape x0 -> x1, local copies, waits for them, and re-layouts: none -> 12.6 us  [shards(): jnp.concatenate(lax.all_to_all(jnp.stack([packed] * lax.axis_size(axes)),...]
    unnamed x11 -> x10, local copies, waits for them, and re-layouts: 12.6 us -> 0.02 us
    all_to_all x0 -> x1, starting transfers between devices: none -> 11.6 us  [shards(): lax.all_to_all(jnp.stack([packed] * lax.axis_size(axes)), axes, 0, 0)]
    reduce_scatter x1, waiting for transfers between devices: 659 us -> 670 us  [shards(): lax.psum_scatter(terms, axes, scatter_dimension=0, tiled=False)]
where the time goes in v1:
time: 871 us; the launch traced here: 870 us
  waiting for transfers between devices  777 us (89%)
  local copies, waits for them, and re-layouts  33.2 us (4%)
  matrix products  27.3 us (3%)
  starting transfers between devices  15 us (2%)
  between operations  13.5 us (2%)
    reduce_scatter x1, waiting for transfers between devices, shards(): lax.psum_scatter(terms, axes, scatter_dimension=0, tiled=False)  670 us
    all_to_all x1, waiting for transfers between devices, shards(): lax.all_to_all(jnp.stack([packed] * lax.axis_size(axes)), axes, 0, 0)  103 us
  transfers between devices with their start and end apart: 3, of which 3 were waited for; matrix products, arithmetic and copies ran while one was open for 0% of the time, Pallas kernels for 0%

profile of v1, /device:TPU:0, one launch (start us, length us, event | category | flops | bytes accessed | tf_op | source)
XLA Modules:
  0.0 869.6 jit_solution(441742927683370989)
XLA Ops:
  6.5 0.9 iota_compare_fusion.1
  7.4 0.8 bitcast_convert_fusion
  8.2 1.0 fusion.41
  9.2 2.4 fusion.49
  11.6 0.2 fusion.36
  11.9 0.5 fusion.33
  12.4 0.7 convert_element_type.71
  13.0 3.3 all-to-all-start
  16.3 0.1 fusion.44
  16.5 4.0 all-to-all-done
  20.5 0.2 multiply_reduce_fusion
  20.7 0.1 multiply_convert_fusion
  20.8 5.5 stack.2
  26.3 11.6 %all-to-all-start.1 = ((bf16[128,4,8320]{2,1,0:T(4,128)(2,1)}), bf16[128,4,8320]{2,1,0:T(4,128)(2,1)}, u32[]{:S(2)}, u32[]{:S(2)}) async-start(bf16[128,4,8320]{2,1,0:T(4,128)(2,1)} %stack.2), calls=%async_computation.1 | async-start | bytes 17039360 | tf_op jit(solution)/shard_map/all_to_all | solution.py:75
  37.9 0.0 reduce-scatter.2.cloned.1.call-start
  38.0 102.9 %all-to-all-done.1 = bf16[128,4,8320]{2,1,0:T(4,128)(2,1)} async-done(((bf16[128,4,8320]{2,1,0:T(4,128)(2,1)}), bf16[128,4,8320]{2,1,0:T(4,128)(2,1)}, u32[]{:S(2)}, u32[]{:S(2)}) %all-to-all-start.1) | async-done | bytes 8519712 | tf_op jit(solution)/shard_map/all_to_all | solution.py:75
  140.9 12.6 %reshape.81 = bf16[512,8320]{1,0:T(8,128)(2,1)} reshape(bf16[128,4,8320]{2,1,0:T(4,128)(2,1)} %all-to-all-done.1) | data formatting | bytes 17039360 | tf_op jit(solution)/shard_map/reshape | solution.py:74
  153.5 1.0 select_reduce_fusion
  154.5 6.3 fusion
  160.8 17.2 %convolution_convert_fusion = bf16[512,8192]{1,0:T(8,128)(2,1)} fusion(bf16[128,8192]{1,0:T(8,128)(2,1)S(1)} %copy-done, f32[512,128]{1,0:T(8,128)S(1)} %fusion, bf16[8192,128]{1,0:T(8,128)(2,1)} %param.21, bf16[512,8320]{1,0:T(8,128)(2,1)} %reshape.81, f32[512]{0:T(512)S(1)} %select_reduce_fusion), kind=kOutput, calls=%fused_computation | convolution fusion | flops 2151940096 | bytes 21235712 | tf_op jit(solution)/shard_map/dot_general | solution.py:84
  178.0 13.5 %reshape.82 = bf16[128,32,1024]{2,1,0:T(8,128)(2,1)} reshape(bf16[512,8192]{1,0:T(8,128)(2,1)} %convolution_convert_fusion) | data formatting | bytes 16777216 | tf_op jit(solution)/shard_map/reshape | solution.py:85
  191.5 669.6 %reduce-scatter.2.cloned.1.call-done = bf16[1,32,1024]{2,1,0:T(8,128)(2,1)} async-done(((bf16[128,32,1024]{2,1,0:T(8,128)(2,1)}), bf16[1,32,1024]{2,1,0:T(8,128)(2,1)}) %reduce-scatter.2.cloned.1.call-update) | async-done | bytes 65552 | tf_op jit(solution)/shard_map/reduce_scatter | solution.py:86
  861.1 0.9 reshape.85
  862.1 0.7 add_convert_fusion
  (19 shorter events, 0.2 us)
Async XLA Ops:
  6.5 154.3 %copy-start = (bf16[128,8192]{1,0:T(8,128)(2,1)S(1)}, bf16[128,8192]{1,0:T(8,128)(2,1)}, u32[]{:S(2)}) copy-start(bf16[128,8192]{1,0:T(8,128)(2,1)} %param.23) | copy-start | bytes 6291460
  6.5 5.4 copy-start.4
  11.6 4.7 copy-start.3
  11.8 8.6 copy-start.1
  11.9 8.8 %copy-start.2 = (f32[8192]{0:T(1024)S(1)}, f32[8192]{0:T(1024)}, u32[]{:S(2)}) copy-start(f32[8192]{0:T(1024)} %param.19) | copy-start | bytes 98308
  13.0 7.4 all-to-all-start
  26.3 114.6 %all-to-all-start.1 = ((bf16[128,4,8320]{2,1,0:T(4,128)(2,1)}), bf16[128,4,8320]{2,1,0:T(4,128)(2,1)}, u32[]{:S(2)}, u32[]{:S(2)}) async-start(bf16[128,4,8320]{2,1,0:T(4,128)(2,1)} %stack.2), calls=%async_computation.1 | async-start | bytes 17039360 | tf_op jit(solution)/shard_map/all_to_all | solution.py:75
  37.9 823.2 %reduce-scatter.2.cloned.1.call-start = ((), (), s32[]{:S(2)}) async-start(), calls=%async_computation.3 | async-start | bytes 8454144 | tf_op jit(solution)/shard_map/reduce_scatter | solution.py:86
Sparse Core Ops, SparseCore 0:
  191.6 669.4 reduce-scatter.1
